TPU v7x, 32 devices: a whole 2x2x4 slice. The times are simulated.
32 devices in a mesh: groups: 2 (over x), seq: 16 (over z, y, core).
Axes of the slice: x: 2, y: 2, z: 4, core: 2. Of those that a mesh axis runs over, the one named last changes fastest.
Arguments:
- enc_input: bfloat16 [8192, 1408], P(('groups', 'seq')), parts along dimension 0, may hold values from -6 to 6
- enc_weight: bfloat16 [2816, 1536], P('seq'), may hold values from -0.109375 to 0.109375
- norm_gain: float32 [1536], replicated, may hold values from 0.5 to 1.5
- q_weight: bfloat16 [1536, 1024], replicated, may hold values from -1 to 1
- kv_weight: bfloat16 [1536, 320], replicated, may hold values from -1 to 1
- out_weight: bfloat16 [1536, 1536], replicated, may hold values from -0.15625 to 0.15625
- dec_weight: float32 [3, 1536], replicated, may hold values from -3 to 3
- track_weight: bfloat16 [192, 1536], P('seq'), may hold values from -0.15625 to 0.15625
- track_grad: bfloat16 [4096, 192], P('groups', 'seq'), parts along dimension 0, may hold values from -6 to 6
- track_index: int32 [384], P('groups'), parts along dimension 0, may hold values from 0 to 191, each once
- track_mask: int32 [384], P('groups'), parts along dimension 0, may hold values 0 or 1
Outputs:
- trunk_out: bfloat16 [4096, 1536], P(('groups', 'seq')), parts along dimension 0
- skip_grad: bfloat16 [4096, 1536], P(('groups', 'seq')), parts along dimension 0
- dec_weight_grad: float32 [6, 1536], P('groups'), parts along dimension 0
There are 2 independent parts, one for each index of `groups`. A program takes and returns all parts, laid end to end along the dimension named above; an argument that names none is the same for every part. Nothing has to cross between parts.
Inputs may be any that keep to these rules, and one draw needn't show every extreme that they name: `track_index`: names every track once.
All inputs are finite; a program needn't handle non-finite values.
Results may differ from a plain program's by a relative error of at most 0.02.
Values may be sent and summed in bfloat16 or wider, within the bound.
No kernel may reach another device: no remote copies, remote signals or barrier semaphores. Data moves between devices by JAX's collectives and lax.ppermute only.
A program may use at most 128 MiB of HBM per device.

v0:
```python
import math
import jax
import jax.numpy as jnp
from jax import lax
from jax.sharding import PartitionSpec as P

HEADS = 8
QK = 128
VDIM = 192
DILATION_SPAN = 8


def with_halo(cells, sides, width):
    for axis, dim in sides:
        count = lax.axis_size(axis)
        ends = count - 1
        head = lax.slice_in_dim(cells, 0, width, axis=dim)
        tail = lax.slice_in_dim(cells, cells.shape[dim] - width, cells.shape[dim], axis=dim)
        cells = jnp.concatenate(
            [
                lax.ppermute(tail, axis, [(i, (i + 1) % count) for i in range(ends)]),
                cells,
                lax.ppermute(head, axis, [((i + 1) % count, i) for i in range(ends)]),
            ],
            axis=dim,
        )
    return cells


def gelu_tanh(values):
    return jax.nn.gelu(values, approximate=True)


def attention(tokens, tok_f, norm_gain, q_weight, kv_weight, out_weight):
    token_rows = tokens.shape[0]
    normed = (
        tok_f * lax.rsqrt(jnp.mean(tok_f * tok_f, axis=-1, keepdims=True) + 1e-06) * norm_gain
    ).astype(jnp.bfloat16)
    query = jnp.dot(normed, q_weight, preferred_element_type=jnp.float32).astype(jnp.bfloat16)
    keyval = jnp.dot(normed, kv_weight, preferred_element_type=jnp.float32).astype(jnp.bfloat16)
    query_rows = query.reshape(token_rows * HEADS, QK)

    def block_update(carry, key_block):
        running_max, running_sum, weighted = carry
        scores = lax.dot_general(
            query_rows,
            key_block[:, :QK],
            (((1,), (1,)), ((), ())),
            preferred_element_type=jnp.float32,
        ) * QK ** (-0.5)
        new_max = jnp.maximum(running_max, jnp.max(scores, axis=1))
        shrink = jnp.exp(running_max - new_max)
        expw = jnp.exp(scores - new_max[:, None])
        running_sum = running_sum * shrink + jnp.sum(expw, axis=1)
        weighted = weighted * shrink[:, None] + jnp.dot(
            expw.astype(jnp.bfloat16), key_block[:, QK:], preferred_element_type=jnp.float32
        )
        return (new_max, running_sum, weighted)

    start_state = (
        jnp.full((token_rows * HEADS,), -1e30, jnp.float32),
        jnp.zeros((token_rows * HEADS,), jnp.float32),
        jnp.zeros((token_rows * HEADS, VDIM), jnp.float32),
    )
    carry = start_state
    piece = lax.all_gather(keyval, "seq", axis=0, tiled=True)
    count = piece.shape[0]

    def step_fn(inner, key_block):
        return (block_update(inner, key_block), 0)

    carry, unused = lax.scan(step_fn, carry, piece.reshape(count // 128, 128, piece.shape[1]))
    running_max, running_sum, weighted = carry
    context = (
        (weighted / running_sum[:, None]).reshape(token_rows, HEADS * VDIM).astype(jnp.bfloat16)
    )
    return (tok_f + jnp.dot(context, out_weight, preferred_element_type=jnp.float32)).astype(
        jnp.bfloat16
    )


def decoder_back(tok_f, dec_weight, track_weight, track_grad, track_index, track_mask):
    token_rows = tok_f.shape[0]
    exchanged = lax.all_to_all(track_grad, "seq", split_axis=0, concat_axis=1, tiled=True)
    masked = exchanged * track_mask.astype(jnp.bfloat16)[None, :]
    every_row = lax.all_gather(track_weight, "seq", axis=0, tiled=True)
    selected = jnp.take(every_row, track_index, axis=0)
    head_f = jnp.dot(masked, selected, preferred_element_type=jnp.float32)
    head_gradient = head_f.astype(jnp.bfloat16)
    padded_input = with_halo(head_gradient, (("seq", 0),), DILATION_SPAN).astype(jnp.float32)
    skip_act, pullback = jax.vjp(gelu_tanh, tok_f)
    convback = jnp.zeros(tok_f.shape, jnp.float32)
    tap_terms = []
    for shift_amount in range(3):
        shifted_rows = padded_input[
            DILATION_SPAN * (2 - shift_amount) : DILATION_SPAN * (2 - shift_amount) + token_rows
        ]
        convback = convback + dec_weight[shift_amount][None, :] * shifted_rows
        tap_terms.append(jnp.sum(skip_act * shifted_rows, axis=0))
    skip_grad = pullback(convback)[0].astype(jnp.bfloat16)
    summed = lax.psum(jnp.stack(tap_terms, axis=0), "seq")
    dec_weight_grad = summed / jnp.float32(math.sqrt(token_rows * lax.axis_size("seq")))
    return (skip_grad, dec_weight_grad)


def shards(
    enc_input,
    enc_weight,
    norm_gain,
    q_weight,
    kv_weight,
    out_weight,
    dec_weight,
    track_weight,
    track_grad,
    track_index,
    track_mask,
):
    token_rows = enc_input.shape[0] // 2
    patches = enc_input.reshape(token_rows, 2 * enc_input.shape[1])
    tok_sum = jnp.dot(
        patches,
        lax.all_gather(enc_weight, "seq", axis=0, tiled=True),
        preferred_element_type=jnp.float32,
    )
    tokens = tok_sum.astype(jnp.bfloat16)
    tok_f = tokens.astype(jnp.float32)
    trunk_out = attention(tokens, tok_f, norm_gain, q_weight, kv_weight, out_weight)
    skip_grad, dec_weight_grad = decoder_back(
        tok_f, dec_weight, track_weight, track_grad, track_index, track_mask
    )
    return (trunk_out, skip_grad, dec_weight_grad)


def solution(mesh):
    return jax.shard_map(
        shards,
        mesh=mesh,
        in_specs=(
            P(("groups", "seq"), None),
            P("seq", None),
            P(),
            P(),
            P(),
            P(),
            P(),
            P("seq", None),
            P("groups", "seq"),
            P("groups"),
            P("groups"),
        ),
        out_specs=(P(("groups", "seq"), None), P(("groups", "seq"), None), P("groups", None)),
        check_vma=False,
    )
```

profile of v0, /device:TPU:0, one launch (start us, length us, event | category | flops | bytes accessed | tf_op | source)
XLA Modules:
  0.0 272.7 jit_solution(8789962556055584525)
XLA Ops:
  9.6 7.4 %all-to-all-start = ((bf16[16,128,12]{1,2,0:T(8,128)(2,1)}), bf16[16,128,12]{1,2,0:T(8,128)(2,1)S(1)}, u32[]{:S(2)}, u32[]{:S(2)}) async-start(bf16[16,128,12]{1,2,0:T(8,128)(2,1)} %copy.20), calls=%async_computation | async-start | bytes 131072 | tf_op jit(solution)/shard_map/all_to_all | solution.py:84
  17.1 30.1 %all-gather = bf16[16,12,1536]{2,1,0:T(8,128)(2,1)} all-gather(bf16[1,12,1536]{2,1,0:T(8,128)(2,1)} %bitcast.28), channel_id=1, replica_groups=mesh['groups'=2,'seq'=16] {'seq'}, dimensions={0}, use_global_device_ids=true | all-gather | bytes 626688 | tf_op jit(solution)/shard_map/all_gather | solution.py:86
  51.3 3.6 %gather_fusion = bf16[192,1536]{1,0:T(8,128)(2,1)} fusion(bf16[192,1536]{1,0:T(8,128)(2,1)} %reshape.51, s32[1024]{0:T(1024)S(1)} %pad_clamp_fusion), kind=kCustom, calls=%fused_computation | custom fusion | bytes 1180416 | tf_op jit(solution)/shard_map/jit(_take)/gather | solution.py:87
  57.7 2.8 %collective-permute-start = (bf16[8,1536]{1,0:T(8,128)(2,1)}, bf16[8,1536]{1,0:T(8,128)(2,1)}, u32[]{:S(2)}, u32[]{:S(2)}) collective-permute-start(bf16[8,1536]{1,0:T(8,128)(2,1)} %get-tuple-element.101), channel_id=1, source_target_pairs={{0,1},{1,2},{2,3},{3,4},{4,5},{5,6},{6,7},{7,8},{8,9},{9,10},{10,1... | collective-permute-start | bytes 73736 | tf_op jit(solution)/shard_map/ppermute | solution.py:21
  67.2 26.1 %all-gather.4.cloned.1.call-done = bf16[2816,1536]{1,0:T(8,128)(2,1)} async-done(((bf16[176,1536]{1,0:T(8,128)(2,1)}), bf16[2816,1536]{1,0:T(8,128)(2,1)}) %all-gather.4.cloned.1.call-update) | async-done | bytes 8650768 | tf_op jit(solution)/shard_map/all_gather | solution.py:123
  93.3 7.5 %multiply_reduce_fusion.3 = (f32[1536]{0:T(1024)S(1)}, f32[1536]{0:T(1024)S(1)}, f32[1536]{0:T(1024)S(1)}, f32[128]{0:T(128)S(1)}, bf16[128,1536]{1,0:T(8,128)(2,1)}, /*index=5*/f32[128,1536]{1,0:T(8,128)S(1)}) fusion(f32[144,1536]{1,0:T(8,128)} %maximum_convert_fusion, f32[1536]{0:T(1024)S(1)} %get-tuple-element.82, f32[1536]{0:T(1024)} %get-tuple-element.83, ...), kind=kOutput, calls=%fused_computation.34 | convolution fusion | flops 1114172800 | bytes 12947968 | tf_op jit(solution)/shard_map/dot_general | solution.py:121
  106.4 59.2 %psum.7 = f32[3,1536]{1,0:T(4,128)S(1)} all-reduce(f32[3,1536]{1,0:T(4,128)S(1)} %pad_maximum_fusion), channel_id=1, replica_groups=mesh['groups'=2,'seq'=16] {'seq'}, use_global_device_ids=true, to_apply=%region_8.9 | all-reduce | flops 4608 | bytes 36864 | tf_op jit(solution)/shard_map/psum | solution.py:101
  166.2 2.6 copy.21
  168.7 89.4 %while.15 = (s32[]{:T(128)}, f32[1024]{0:T(1024)S(1)}, f32[1024]{0:T(1024)S(1)}, f32[1024,192]{0,1:T(8,128)}, bf16[16,128,320]{2,1,0:T(8,128)(2,1)}, /*index=5*/bf16[1024,128]{1,0:T(8,128)(2,1)S(1)}, s32[]{:T(128)}, s32[]{:T(128)}) while((s32[]{:T(128)}, f32[1024]{0:T(1024)S(1)}, f32[1024]{0:T(1024)S(1)}, f32[1024,192]{0,1:T(8,128)}, ...), condition=%wide.region_4.5_spmd.clone, body=%wide.region_1.4_spmd.clone.sunk | while | flops 85267456 | bytes 3735653 | solution.py:72
  177.2 2.5 convolution_add_fusion.3
  182.8 2.5 convolution_add_fusion.3
  188.4 2.5 convolution_add_fusion.3
  194.0 2.5 convolution_add_fusion.3
  199.6 2.5 convolution_add_fusion.3
  205.2 2.5 convolution_add_fusion.3
  210.8 2.5 convolution_add_fusion.3
  216.4 2.5 convolution_add_fusion.3
  222.0 2.5 convolution_add_fusion.3
  227.6 2.5 convolution_add_fusion.3
  233.2 2.5 convolution_add_fusion.3
  238.8 2.5 convolution_add_fusion.3
  244.4 2.5 convolution_add_fusion.3
  250.0 2.5 convolution_add_fusion.3
  261.8 4.1 %fusion.8 = bf16[128,1536]{1,0:T(8,128)(2,1)} fusion(f32[128,1536]{1,0:T(8,128)} %copy-done.1, bf16[128,1536]{1,0:T(8,128)(2,1)S(1)} %convert_element_type.46, bf16[1536,1536]{1,0:T(8,128)(2,1)} %param.18), kind=kOutput, calls=%fused_computation.19 | convolution fusion | flops 604372992 | bytes 6291456 | tf_op jit(solution)/shard_map/dot_general | solution.py:77
  (144 shorter events, 80.2 us)
Async XLA Ops:
  7.2 95.6 %copy-start = (bf16[1536,1024]{1,0:T(8,128)(2,1)S(1)}, bf16[1536,1024]{1,0:T(8,128)(2,1)}, u32[]{:S(2)}) copy-start(bf16[1536,1024]{1,0:T(8,128)(2,1)} %param.16) | copy-start | bytes 9437188
  7.2 86.1 %all-gather.4.cloned.1.call-start = ((), (), s32[]{:S(2)}) async-start(), calls=%async_computation.1 | async-start | bytes 9191424 | tf_op jit(solution)/shard_map/all_gather | solution.py:123
  9.6 45.3 %all-to-all-start = ((bf16[16,128,12]{1,2,0:T(8,128)(2,1)}), bf16[16,128,12]{1,2,0:T(8,128)(2,1)S(1)}, u32[]{:S(2)}, u32[]{:S(2)}) async-start(bf16[16,128,12]{1,2,0:T(8,128)(2,1)} %copy.20), calls=%async_computation | async-start | bytes 131072 | tf_op jit(solution)/shard_map/all_to_all | solution.py:84
  17.0 149.2 %all-gather.6.cloned.1.call-start = ((), (), s32[]{:S(2)}) async-start(), calls=%async_computation.2 | async-start | bytes 1392640 | tf_op jit(solution)/shard_map/all_gather | solution.py:66
  57.7 7.7 %collective-permute-start = (bf16[8,1536]{1,0:T(8,128)(2,1)}, bf16[8,1536]{1,0:T(8,128)(2,1)}, u32[]{:S(2)}, u32[]{:S(2)}) collective-permute-start(bf16[8,1536]{1,0:T(8,128)(2,1)} %get-tuple-element.101), channel_id=1, source_target_pairs={{0,1},{1,2},{2,3},{3,4},{4,5},{5,6},{6,7},{7,8},{8,9},{9,10},{10,1... | collective-permute-start | bytes 73736 | tf_op jit(solution)/shard_map/ppermute | solution.py:21
  60.5 4.9 %collective-permute-start.1 = (bf16[8,1536]{1,0:T(8,128)(2,1)}, bf16[8,1536]{1,0:T(8,128)(2,1)}, u32[]{:S(2)}, u32[]{:S(2)}) collective-permute-start(bf16[8,1536]{1,0:T(8,128)(2,1)} %get-tuple-element.102), channel_id=1, source_target_pairs={{1,0},{2,1},{3,2},{4,3},{5,4},{6,5},{7,6},{8,7},{9,8},{10,9},{11,1... | collective-permute-start | bytes 73736 | tf_op jit(solution)/shard_map/ppermute | solution.py:23
  93.3 8.3 %copy-start.2 = (bf16[1536,320]{0,1:T(8,128)(2,1)S(1)}, bf16[1536,320]{0,1:T(8,128)(2,1)}, u32[]{:S(2)}) copy-start(bf16[1536,320]{0,1:T(8,128)(2,1)} %param.17) | copy-start | bytes 2949124
  93.3 8.3 %copy-start.3 = (f32[1536]{0:T(1024)S(1)}, f32[1536]{0:T(1024)}, u32[]{:S(2)}) copy-start(f32[1536]{0:T(1024)} %param.15) | copy-start | bytes 18436
  100.7 0.9 copy-start.1
Sparse Core Ops, SparseCore 0:
  10.3 82.9 all-gather.3
  102.9 36.2 all-gather.5
where the time goes:
time: 275 us; the launch traced here: 273 us
  blocking collectives  89.3 us (32%)
  matrix products  72.9 us (27%)
  local copies, waits for them, and re-layouts  33.7 us (12%)
  waiting for transfers between devices  26.8 us (10%)
  other arithmetic  24.2 us (9%)
  between operations  14.2 us (5%)
  starting transfers between devices  11.6 us (4%)
    psum x1, blocking collectives, decoder_back(): summed = lax.psum(jnp.stack(tap_terms, axis=0), 'seq')  59.2 us
    dot_general x16, matrix products, block_update(): jnp.dot(expw.astype(jnp.bfloat16), key_block[:, QK:], preferred_element_t...  39.6 us
    all_gather x1, blocking collectives, decoder_back(): every_row = lax.all_gather(track_weight, 'seq', axis=0, tiled=True)  30.1 us
    all_gather x1, waiting for transfers between devices, shards(): lax.all_gather(enc_weight, 'seq', axis=0, tiled=True)  26.1 us
    reduce_sum x16, other arithmetic, block_update(): running_sum = running_sum * shrink + jnp.sum(expw, axis=1)  18.2 us
    dot_general x16, matrix products, block_update(): lax.dot_general(query_rows, key_block[:, :QK], (((1,), (1,)), ((), ())),...  16.7 us
    squeeze x16, local copies, waits for them, and re-layouts, attention(): lax.scan(step_fn, carry, piece.reshape(count // 128, 128, piece.shape[1]))  14.4 us
    dot_general x1, matrix products, shards(): jnp.dot(patches, lax.all_gather(enc_weight, 'seq', axis=0, tiled=True), p...  7.46 us
  transfers between devices with their start and end apart: 5, of which 1 were waited for; matrix products, arithmetic and copies ran while one was open for 8% of the time, Pallas kernels for 0%

commit v1 on v0

--- a/solution.py
+++ b/solution.py
@@ -98,7 +98,9 @@
         convback = convback + dec_weight[shift_amount][None, :] * shifted_rows
         tap_terms.append(jnp.sum(skip_act * shifted_rows, axis=0))
     skip_grad = pullback(convback)[0].astype(jnp.bfloat16)
-    summed = lax.psum(jnp.stack(tap_terms, axis=0), "seq")
+    block = jnp.stack(tap_terms, axis=0)
+    pieces = lax.all_gather(block, "seq", axis=0, tiled=False)
+    summed = pieces.sum(axis=0)
     dec_weight_grad = summed / jnp.float32(math.sqrt(token_rows * lax.axis_size("seq")))
     return (skip_grad, dec_weight_grad)
 

time: 275 us -> 249 us (0.905)
  blocking collectives: 89.3 us -> 52 us
  waiting for transfers between devices: 26.8 us -> 36.2 us
    psum x1 -> x0, blocking collectives: 59.2 us -> none  [decoder_back(): summed = lax.psum(jnp.stack(tap_terms, axis=0), 'seq')]
    all_gather x0 -> x1, blocking collectives: none -> 21.9 us  [decoder_back(): pieces = lax.all_gather(block, 'seq', axis=0, tiled=False)]
    all_gather x1, waiting for transfers between devices: 0.01 us -> 9.47 us  [attention(): piece = lax.all_gather(keyval, 'seq', axis=0, tiled=True)]
  transfers between devices with their start and end apart: 5 -> 5, of which waited for: 1 -> 2; matrix products, arithmetic and copies ran while one was open for 8% -> 9% of each run, Pallas kernels for 0% -> 0%
where the time goes in v1:
time: 249 us; the launch traced here: 246 us
  matrix products  73 us (29%)
  blocking collectives  52 us (21%)
  waiting for transfers between devices  36.2 us (15%)
  local copies, waits for them, and re-layouts  33.7 us (14%)
  other arithmetic  25.2 us (10%)
  between operations  14.2 us (6%)
  starting transfers between devices  11.6 us (5%)
    dot_general x16, matrix products, block_update(): jnp.dot(expw.astype(jnp.bfloat16), key_block[:, QK:], preferred_element_t...  39.7 us
    all_gather x1, blocking collectives, decoder_back(): every_row = lax.all_gather(track_weight, 'seq', axis=0, tiled=True)  30.1 us
    all_gather x1, waiting for transfers between devices, shards(): lax.all_gather(enc_weight, 'seq', axis=0, tiled=True)  26.1 us
    all_gather x1, blocking collectives, decoder_back(): pieces = lax.all_gather(block, 'seq', axis=0, tiled=False)  21.9 us
    reduce_sum x16, other arithmetic, block_update(): running_sum = running_sum * shrink + jnp.sum(expw, axis=1)  18.2 us
    dot_general x16, matrix products, block_update(): lax.dot_general(query_rows, key_block[:, :QK], (((1,), (1,)), ((), ())),...  16.7 us
    squeeze x16, local copies, waits for them, and re-layouts, attention(): lax.scan(step_fn, carry, piece.reshape(count // 128, 128, piece.shape[1]))  14.4 us
    all_gather x1, waiting for transfers between devices, attention(): piece = lax.all_gather(keyval, 'seq', axis=0, tiled=True)  9.47 us
  transfers between devices with their start and end apart: 5, of which 2 were waited for; matrix products, arithmetic and copies ran while one was open for 9% of the time, Pallas kernels for 0%

profile of v1, /device:TPU:0, one launch (start us, length us, event | category | flops | bytes accessed | tf_op | source)
XLA Modules:
  0.0 246.1 jit_solution(6367389038292693644)
XLA Ops:
  9.6 7.4 %all-to-all-start = ((bf16[16,128,12]{1,2,0:T(8,128)(2,1)}), bf16[16,128,12]{1,2,0:T(8,128)(2,1)S(1)}, u32[]{:S(2)}, u32[]{:S(2)}) async-start(bf16[16,128,12]{1,2,0:T(8,128)(2,1)} %copy.20), calls=%async_computation | async-start | bytes 131072 | tf_op jit(solution)/shard_map/all_to_all | solution.py:84
  17.1 30.1 %all-gather.1 = bf16[16,12,1536]{2,1,0:T(8,128)(2,1)} all-gather(bf16[1,12,1536]{2,1,0:T(8,128)(2,1)} %bitcast.30), channel_id=1, replica_groups=mesh['groups'=2,'seq'=16] {'seq'}, dimensions={0}, use_global_device_ids=true | all-gather | bytes 626688 | tf_op jit(solution)/shard_map/all_gather | solution.py:86
  51.3 3.6 %gather_fusion = bf16[192,1536]{1,0:T(8,128)(2,1)} fusion(bf16[192,1536]{1,0:T(8,128)(2,1)} %reshape.52, s32[1024]{0:T(1024)S(1)} %pad_clamp_fusion), kind=kCustom, calls=%fused_computation | custom fusion | bytes 1180416 | tf_op jit(solution)/shard_map/jit(_take)/gather | solution.py:87
  57.7 2.8 %collective-permute-start = (bf16[8,1536]{1,0:T(8,128)(2,1)}, bf16[8,1536]{1,0:T(8,128)(2,1)}, u32[]{:S(2)}, u32[]{:S(2)}) collective-permute-start(bf16[8,1536]{1,0:T(8,128)(2,1)} %get-tuple-element.101), channel_id=1, source_target_pairs={{0,1},{1,2},{2,3},{3,4},{4,5},{5,6},{6,7},{7,8},{8,9},{9,10},{10,1... | collective-permute-start | bytes 73736 | tf_op jit(solution)/shard_map/ppermute | solution.py:21
  67.2 26.1 %all-gather.6.cloned.1.call-done = bf16[2816,1536]{1,0:T(8,128)(2,1)} async-done(((bf16[176,1536]{1,0:T(8,128)(2,1)}), bf16[2816,1536]{1,0:T(8,128)(2,1)}) %all-gather.6.cloned.1.call-update) | async-done | bytes 8650768 | tf_op jit(solution)/shard_map/all_gather | solution.py:125
  93.3 7.5 %multiply_reduce_fusion.3 = (f32[1536]{0:T(1024)S(1)}, f32[1536]{0:T(1024)S(1)}, f32[1536]{0:T(1024)S(1)}, f32[128]{0:T(128)S(1)}, bf16[128,1536]{1,0:T(8,128)(2,1)}, /*index=5*/f32[128,1536]{1,0:T(8,128)S(1)}) fusion(f32[144,1536]{1,0:T(8,128)} %maximum_convert_fusion, f32[1536]{0:T(1024)S(1)} %get-tuple-element.82, f32[1536]{0:T(1024)} %get-tuple-element.83, ...), kind=kOutput, calls=%fused_computation.34 | convolution fusion | flops 1114172800 | bytes 12947968 | tf_op jit(solution)/shard_map/dot_general | solution.py:123
  106.4 21.9 %all-gather.2 = f32[16,3,1536]{2,1,0:T(4,128)} all-gather(f32[1,3,1536]{2,1,0:T(4,128)S(1)} %maximum_bitcast_fusion), channel_id=2, replica_groups=mesh['groups'=2,'seq'=16] {'seq'}, dimensions={0}, use_global_device_ids=true | all-gather | bytes 313344 | tf_op jit(solution)/shard_map/all_gather | solution.py:102
  130.0 9.5 %all-gather.8.cloned.1.call-done = bf16[2048,320]{0,1:T(8,128)(2,1)} async-done(((bf16[128,320]{0,1:T(8,128)(2,1)}), bf16[2048,320]{0,1:T(8,128)(2,1)}) %all-gather.8.cloned.1.call-update) | async-done | bytes 1310736 | tf_op jit(solution)/shard_map/all_gather | solution.py:66
  139.5 2.6 %copy.21 = bf16[2048,320]{1,0:T(8,128)(2,1)} copy(bf16[2048,320]{0,1:T(8,128)(2,1)} %all-gather.8.cloned.1.call-done) | data formatting | bytes 2621440
  142.0 89.4 %while.15 = (s32[]{:T(128)}, f32[1024]{0:T(1024)S(1)}, f32[1024]{0:T(1024)S(1)}, f32[1024,192]{0,1:T(8,128)}, bf16[16,128,320]{2,1,0:T(8,128)(2,1)}, /*index=5*/bf16[1024,128]{1,0:T(8,128)(2,1)S(1)}, s32[]{:T(128)}, s32[]{:T(128)}) while((s32[]{:T(128)}, f32[1024]{0:T(1024)S(1)}, f32[1024]{0:T(1024)S(1)}, f32[1024,192]{0,1:T(8,128)}, ...), condition=%wide.region_4.5_spmd.clone, body=%wide.region_1.4_spmd.clone.sunk | while | flops 85267456 | bytes 3735653 | solution.py:72
  150.5 2.5 %convolution_add_fusion.3 = f32[1024,192]{0,1:T(8,128)} fusion(f32[1024,192]{0,1:T(8,128)} %get-tuple-element.160, f32[1024]{0:T(1024)S(1)} %get-tuple-element.148, pred[]{:T(512)S(6)} %compare.3, f32[128,1024]{1,0:T(8,128)} %get-tuple-element.146, f32[1024]{0:T(1024)S(1)} %select_maximum_fusion.2, bf16[128,320]{1,0:T(8,128)(2,1)S(1)} %dynamic-slice_bitcast_fusion.2), kind=kOutput, calls=%fused_computation.1.clone.1 | convolution fusion | flops 51183616 | bytes 2170881 | tf_op jit(solution)/shard_map/while/body/eval_jaxpr/dot_general | solution.py:55
  156.1 2.5 %convolution_add_fusion.3 = f32[1024,192]{0,1:T(8,128)} fusion(f32[1024,192]{0,1:T(8,128)} %get-tuple-element.160, f32[1024]{0:T(1024)S(1)} %get-tuple-element.148, pred[]{:T(512)S(6)} %compare.3, f32[128,1024]{1,0:T(8,128)} %get-tuple-element.146, f32[1024]{0:T(1024)S(1)} %select_maximum_fusion.2, bf16[128,320]{1,0:T(8,128)(2,1)S(1)} %dynamic-slice_bitcast_fusion.2), kind=kOutput, calls=%fused_computation.1.clone.1 | convolution fusion | flops 51183616 | bytes 2170881 | tf_op jit(solution)/shard_map/while/body/eval_jaxpr/dot_general | solution.py:55
  161.7 2.5 %convolution_add_fusion.3 = f32[1024,192]{0,1:T(8,128)} fusion(f32[1024,192]{0,1:T(8,128)} %get-tuple-element.160, f32[1024]{0:T(1024)S(1)} %get-tuple-element.148, pred[]{:T(512)S(6)} %compare.3, f32[128,1024]{1,0:T(8,128)} %get-tuple-element.146, f32[1024]{0:T(1024)S(1)} %select_maximum_fusion.2, bf16[128,320]{1,0:T(8,128)(2,1)S(1)} %dynamic-slice_bitcast_fusion.2), kind=kOutput, calls=%fused_computation.1.clone.1 | convolution fusion | flops 51183616 | bytes 2170881 | tf_op jit(solution)/shard_map/while/body/eval_jaxpr/dot_general | solution.py:55
  167.3 2.5 %convolution_add_fusion.3 = f32[1024,192]{0,1:T(8,128)} fusion(f32[1024,192]{0,1:T(8,128)} %get-tuple-element.160, f32[1024]{0:T(1024)S(1)} %get-tuple-element.148, pred[]{:T(512)S(6)} %compare.3, f32[128,1024]{1,0:T(8,128)} %get-tuple-element.146, f32[1024]{0:T(1024)S(1)} %select_maximum_fusion.2, bf16[128,320]{1,0:T(8,128)(2,1)S(1)} %dynamic-slice_bitcast_fusion.2), kind=kOutput, calls=%fused_computation.1.clone.1 | convolution fusion | flops 51183616 | bytes 2170881 | tf_op jit(solution)/shard_map/while/body/eval_jaxpr/dot_general | solution.py:55
  172.9 2.5 %convolution_add_fusion.3 = f32[1024,192]{0,1:T(8,128)} fusion(f32[1024,192]{0,1:T(8,128)} %get-tuple-element.160, f32[1024]{0:T(1024)S(1)} %get-tuple-element.148, pred[]{:T(512)S(6)} %compare.3, f32[128,1024]{1,0:T(8,128)} %get-tuple-element.146, f32[1024]{0:T(1024)S(1)} %select_maximum_fusion.2, bf16[128,320]{1,0:T(8,128)(2,1)S(1)} %dynamic-slice_bitcast_fusion.2), kind=kOutput, calls=%fused_computation.1.clone.1 | convolution fusion | flops 51183616 | bytes 2170881 | tf_op jit(solution)/shard_map/while/body/eval_jaxpr/dot_general | solution.py:55
  178.5 2.5 %convolution_add_fusion.3 = f32[1024,192]{0,1:T(8,128)} fusion(f32[1024,192]{0,1:T(8,128)} %get-tuple-element.160, f32[1024]{0:T(1024)S(1)} %get-tuple-element.148, pred[]{:T(512)S(6)} %compare.3, f32[128,1024]{1,0:T(8,128)} %get-tuple-element.146, f32[1024]{0:T(1024)S(1)} %select_maximum_fusion.2, bf16[128,320]{1,0:T(8,128)(2,1)S(1)} %dynamic-slice_bitcast_fusion.2), kind=kOutput, calls=%fused_computation.1.clone.1 | convolution fusion | flops 51183616 | bytes 2170881 | tf_op jit(solution)/shard_map/while/body/eval_jaxpr/dot_general | solution.py:55
  184.1 2.5 %convolution_add_fusion.3 = f32[1024,192]{0,1:T(8,128)} fusion(f32[1024,192]{0,1:T(8,128)} %get-tuple-element.160, f32[1024]{0:T(1024)S(1)} %get-tuple-element.148, pred[]{:T(512)S(6)} %compare.3, f32[128,1024]{1,0:T(8,128)} %get-tuple-element.146, f32[1024]{0:T(1024)S(1)} %select_maximum_fusion.2, bf16[128,320]{1,0:T(8,128)(2,1)S(1)} %dynamic-slice_bitcast_fusion.2), kind=kOutput, calls=%fused_computation.1.clone.1 | convolution fusion | flops 51183616 | bytes 2170881 | tf_op jit(solution)/shard_map/while/body/eval_jaxpr/dot_general | solution.py:55
  189.7 2.5 %convolution_add_fusion.3 = f32[1024,192]{0,1:T(8,128)} fusion(f32[1024,192]{0,1:T(8,128)} %get-tuple-element.160, f32[1024]{0:T(1024)S(1)} %get-tuple-element.148, pred[]{:T(512)S(6)} %compare.3, f32[128,1024]{1,0:T(8,128)} %get-tuple-element.146, f32[1024]{0:T(1024)S(1)} %select_maximum_fusion.2, bf16[128,320]{1,0:T(8,128)(2,1)S(1)} %dynamic-slice_bitcast_fusion.2), kind=kOutput, calls=%fused_computation.1.clone.1 | convolution fusion | flops 51183616 | bytes 2170881 | tf_op jit(solution)/shard_map/while/body/eval_jaxpr/dot_general | solution.py:55
  195.3 2.5 %convolution_add_fusion.3 = f32[1024,192]{0,1:T(8,128)} fusion(f32[1024,192]{0,1:T(8,128)} %get-tuple-element.160, f32[1024]{0:T(1024)S(1)} %get-tuple-element.148, pred[]{:T(512)S(6)} %compare.3, f32[128,1024]{1,0:T(8,128)} %get-tuple-element.146, f32[1024]{0:T(1024)S(1)} %select_maximum_fusion.2, bf16[128,320]{1,0:T(8,128)(2,1)S(1)} %dynamic-slice_bitcast_fusion.2), kind=kOutput, calls=%fused_computation.1.clone.1 | convolution fusion | flops 51183616 | bytes 2170881 | tf_op jit(solution)/shard_map/while/body/eval_jaxpr/dot_general | solution.py:55
  200.9 2.5 %convolution_add_fusion.3 = f32[1024,192]{0,1:T(8,128)} fusion(f32[1024,192]{0,1:T(8,128)} %get-tuple-element.160, f32[1024]{0:T(1024)S(1)} %get-tuple-element.148, pred[]{:T(512)S(6)} %compare.3, f32[128,1024]{1,0:T(8,128)} %get-tuple-element.146, f32[1024]{0:T(1024)S(1)} %select_maximum_fusion.2, bf16[128,320]{1,0:T(8,128)(2,1)S(1)} %dynamic-slice_bitcast_fusion.2), kind=kOutput, calls=%fused_computation.1.clone.1 | convolution fusion | flops 51183616 | bytes 2170881 | tf_op jit(solution)/shard_map/while/body/eval_jaxpr/dot_general | solution.py:55
  206.5 2.5 %convolution_add_fusion.3 = f32[1024,192]{0,1:T(8,128)} fusion(f32[1024,192]{0,1:T(8,128)} %get-tuple-element.160, f32[1024]{0:T(1024)S(1)} %get-tuple-element.148, pred[]{:T(512)S(6)} %compare.3, f32[128,1024]{1,0:T(8,128)} %get-tuple-element.146, f32[1024]{0:T(1024)S(1)} %select_maximum_fusion.2, bf16[128,320]{1,0:T(8,128)(2,1)S(1)} %dynamic-slice_bitcast_fusion.2), kind=kOutput, calls=%fused_computation.1.clone.1 | convolution fusion | flops 51183616 | bytes 2170881 | tf_op jit(solution)/shard_map/while/body/eval_jaxpr/dot_general | solution.py:55
  217.7 2.5 %convolution_add_fusion.3 = f32[1024,192]{0,1:T(8,128)} fusion(f32[1024,192]{0,1:T(8,128)} %get-tuple-element.160, f32[1024]{0:T(1024)S(1)} %get-tuple-element.148, pred[]{:T(512)S(6)} %compare.3, f32[128,1024]{1,0:T(8,128)} %get-tuple-element.146, f32[1024]{0:T(1024)S(1)} %select_maximum_fusion.2, bf16[128,320]{1,0:T(8,128)(2,1)S(1)} %dynamic-slice_bitcast_fusion.2), kind=kOutput, calls=%fused_computation.1.clone.1 | convolution fusion | flops 51183616 | bytes 2170881 | tf_op jit(solution)/shard_map/while/body/eval_jaxpr/dot_general | solution.py:55
  228.9 2.5 %convolution_add_fusion.3 = f32[1024,192]{0,1:T(8,128)} fusion(f32[1024,192]{0,1:T(8,128)} %get-tuple-element.160, f32[1024]{0:T(1024)S(1)} %get-tuple-element.148, pred[]{:T(512)S(6)} %compare.3, f32[128,1024]{1,0:T(8,128)} %get-tuple-element.146, f32[1024]{0:T(1024)S(1)} %select_maximum_fusion.2, bf16[128,320]{1,0:T(8,128)(2,1)S(1)} %dynamic-slice_bitcast_fusion.2), kind=kOutput, calls=%fused_computation.1.clone.1 | convolution fusion | flops 51183616 | bytes 2170881 | tf_op jit(solution)/shard_map/while/body/eval_jaxpr/dot_general | solution.py:55
  235.1 4.1 %fusion.8 = bf16[128,1536]{1,0:T(8,128)(2,1)} fusion(f32[128,1536]{1,0:T(8,128)} %copy-done.1, bf16[128,1536]{1,0:T(8,128)(2,1)S(1)} %convert_element_type.46, bf16[1536,1536]{1,0:T(8,128)(2,1)} %param.18), kind=kOutput, calls=%fused_computation.19 | convolution fusion | flops 604372992 | bytes 6291456 | tf_op jit(solution)/shard_map/dot_general | solution.py:77
  (145 shorter events, 83.9 us)
Async XLA Ops:
  7.2 95.6 %copy-start = (bf16[1536,1024]{1,0:T(8,128)(2,1)S(1)}, bf16[1536,1024]{1,0:T(8,128)(2,1)}, u32[]{:S(2)}) copy-start(bf16[1536,1024]{1,0:T(8,128)(2,1)} %param.16) | copy-start | bytes 9437188
  7.2 86.1 %all-gather.6.cloned.1.call-start = ((), (), s32[]{:S(2)}) async-start(), calls=%async_computation.1 | async-start | bytes 9191424 | tf_op jit(solution)/shard_map/all_gather | solution.py:125
  9.6 45.3 %all-to-all-start = ((bf16[16,128,12]{1,2,0:T(8,128)(2,1)}), bf16[16,128,12]{1,2,0:T(8,128)(2,1)S(1)}, u32[]{:S(2)}, u32[]{:S(2)}) async-start(bf16[16,128,12]{1,2,0:T(8,128)(2,1)} %copy.20), calls=%async_computation | async-start | bytes 131072 | tf_op jit(solution)/shard_map/all_to_all | solution.py:84
  17.0 122.4 %all-gather.8.cloned.1.call-start = ((), (), s32[]{:S(2)}) async-start(), calls=%async_computation.2 | async-start | bytes 1392640 | tf_op jit(solution)/shard_map/all_gather | solution.py:66
  57.7 7.7 %collective-permute-start = (bf16[8,1536]{1,0:T(8,128)(2,1)}, bf16[8,1536]{1,0:T(8,128)(2,1)}, u32[]{:S(2)}, u32[]{:S(2)}) collective-permute-start(bf16[8,1536]{1,0:T(8,128)(2,1)} %get-tuple-element.101), channel_id=1, source_target_pairs={{0,1},{1,2},{2,3},{3,4},{4,5},{5,6},{6,7},{7,8},{8,9},{9,10},{10,1... | collective-permute-start | bytes 73736 | tf_op jit(solution)/shard_map/ppermute | solution.py:21
  60.5 4.9 %collective-permute-start.1 = (bf16[8,1536]{1,0:T(8,128)(2,1)}, bf16[8,1536]{1,0:T(8,128)(2,1)}, u32[]{:S(2)}, u32[]{:S(2)}) collective-permute-start(bf16[8,1536]{1,0:T(8,128)(2,1)} %get-tuple-element.102), channel_id=1, source_target_pairs={{1,0},{2,1},{3,2},{4,3},{5,4},{6,5},{7,6},{8,7},{9,8},{10,9},{11,1... | collective-permute-start | bytes 73736 | tf_op jit(solution)/shard_map/ppermute | solution.py:23
  93.3 8.3 %copy-start.2 = (bf16[1536,320]{0,1:T(8,128)(2,1)S(1)}, bf16[1536,320]{0,1:T(8,128)(2,1)}, u32[]{:S(2)}) copy-start(bf16[1536,320]{0,1:T(8,128)(2,1)} %param.17) | copy-start | bytes 2949124
  93.3 8.3 %copy-start.3 = (f32[1536]{0:T(1024)S(1)}, f32[1536]{0:T(1024)}, u32[]{:S(2)}) copy-start(f32[1536]{0:T(1024)} %param.15) | copy-start | bytes 18436
  100.7 0.9 copy-start.1
Sparse Core Ops, SparseCore 0:
  10.3 82.9 all-gather.5
  102.9 36.5 all-gather.7
